TPU v7x, 32 devices: a whole 2x2x4 slice. The times are simulated.
32 devices in a mesh: grp: 2 (over y), pair: 4 (over z), aux: 2 (over x), rep: 2 (over core).
Axes of the slice: x: 2, y: 2, z: 4, core: 2. Of those that a mesh axis runs over, the one named last changes fastest.
Arguments:
- three_center: bfloat16 [5120, 4, 8000], P(('grp', 'aux', 'rep', 'pair')), parts along dimension 0, may hold values from -0.050591038 to 0.050591038
- eps_occ: float32 [8], P('grp'), parts along dimension 0, may hold values from -1.2 to -0.4
- eps_virt: float32 [16000], P(('grp', 'pair')), parts along dimension 0, may hold values from 0.2 to 3
- freq: float32 [2], P('grp'), parts along dimension 0, may hold values from 0.2 to 2
Outputs:
- polar: float32 [5120, 2560], P(('grp', 'aux', 'rep'), 'pair'), parts along dimension 0
There are 2 independent parts, one for each index of `grp`. A program takes and returns all parts, laid end to end along the dimension named above; each array names one. Nothing has to cross between parts.
All inputs are finite; a program needn't handle non-finite values.
Results may differ from a plain program's by a relative error of at most 0.0003.
Values may be sent and summed in bfloat16 or wider, within the bound.
A program may use at most 192 MiB of HBM per device.

v0:
```python
import jax
import jax.numpy as jnp
from jax import lax
from jax.sharding import PartitionSpec as P


def local(three_center, eps_occ, eps_virt, freq):
    arrived = lax.all_to_all(three_center, "pair", split_axis=2, concat_axis=0, tiled=True)
    excite = eps_virt[None, :] - eps_occ[:, None]
    weight = 2.0 * excite / (excite * excite + freq[0] * freq[0])
    height = arrived.shape[0]
    scaled = (
        (arrived.astype(jnp.float32) * weight[None, :, :]).astype(jnp.bfloat16).reshape(height, -1)
    )
    plain_rows = arrived.reshape(height, -1)
    partial_sums = lax.dot_general(
        scaled,
        lax.all_gather(plain_rows, ("aux", "rep"), axis=0, tiled=True),
        (((1,), (1,)), ((), ())),
        preferred_element_type=jnp.float32,
    )
    return lax.psum_scatter(partial_sums, "pair", scatter_dimension=1, tiled=True)


def solution(mesh):
    return jax.shard_map(
        local,
        mesh=mesh,
        in_specs=(
            P(("grp", "aux", "rep", "pair"), None, None),
            P("grp"),
            P(("grp", "pair")),
            P("grp"),
        ),
        out_specs=P(("grp", "aux", "rep"), "pair"),
        check_vma=False,
    )
```

profile of v0, /device:TPU:0, one launch (start us, length us, event | category | flops | bytes accessed | tf_op | source)
XLA Modules:
  0.0 865.8 jit_solution(16826013014737475002)
XLA Ops:
  6.5 0.0 copy-start
  6.5 0.0 all-gather.2.cloned.1.call-start
  6.5 32.8 %copy.8 = bf16[160,4,8000]{0,1,2:T(4,128)(2,1)} copy(bf16[160,4,8000]{2,1,0:T(4,128)(2,1)} %param.4) | data formatting | bytes 20480000 | tf_op args[0]
  39.3 367.0 %all_to_all.18 = bf16[160,4,8000]{0,1,2:T(4,128)(2,1)} all-to-all(bf16[160,4,8000]{0,1,2:T(4,128)(2,1)} %copy.8), channel_id=1, replica_groups=mesh['grp'=2,'pair'=4,'aux'=2,'rep'=2] {'pair'}, dimensions={2} | all-to-all | bytes 20480000 | tf_op jit(solution)/shard_map/all_to_all | solution.py:8
  406.3 35.7 %copy.9 = bf16[160,4,4,2000]{3,1,0,2:T(4,128)(2,1)} copy(bf16[160,4,4,2000]{0,1,3,2:T(4,128)(2,1)} %bitcast.4) | data formatting | bytes 20480000 | tf_op jit(solution)/shard_map/all_to_all | solution.py:8
  442.0 0.0 copy-start.2
  442.0 20.3 %all_to_all.16 = bf16[640,8000]{1,0:T(8,128)(2,1)} reshape(bf16[4,160,4,2000]{3,2,1,0:T(4,128)(2,1)} %bitcast.5) | data formatting | bytes 20480000 | tf_op jit(solution)/shard_map/all_to_all | solution.py:8
  462.3 0.0 all-gather.2.cloned.1.call-update
  462.3 0.0 reduce-scatter.2.cloned.1.call-start
  463.0 0.0 copy-done
  463.1 0.1 broadcast_reduce_fusion
  463.2 0.1 sub.24
  463.3 0.0 copy-done.2
  463.3 0.1 sub.22
  463.4 245.1 %all-gather.2.cloned.1.call-done = bf16[2560,8000]{1,0:T(8,128)(2,1)} async-done(((bf16[640,8000]{1,0:T(8,128)(2,1)}), bf16[2560,8000]{1,0:T(8,128)(2,1)}) %all-gather.2.cloned.1.call-update) | async-done | bytes 40960016 | tf_op jit(solution)/shard_map/all_gather | solution.py:18
  708.5 0.0 copy-start.1
  708.5 35.3 %fusion = f32[640,2560]{1,0:T(8,128)} fusion(bf16[2560,8000]{1,0:T(8,128)(2,1)} %all-gather.2.cloned.1.call-done, bf16[640,8000]{1,0:T(8,128)(2,1)} %all_to_all.16, f32[8000]{0:T(1024)S(1)} %add_divide_fusion), kind=kOutput, calls=%fused_computation.1 | convolution fusion | flops 26229760000 | bytes 57785600 | tf_op jit(solution)/shard_map/dot_general | solution.py:16
  743.8 0.0 reduce-scatter.2.cloned.1.call-update
  743.8 115.2 %reduce-scatter.2.cloned.1.call-done = f32[640,640]{1,0:T(8,128)} async-done(((f32[640,2560]{1,0:T(8,128)}), f32[640,640]{1,0:T(8,128)}) %reduce-scatter.2.cloned.1.call-update) | async-done | bytes 1638416 | tf_op jit(solution)/shard_map/reduce_scatter | solution.py:22
  859.0 0.0 copy-done.1
  (2 shorter events, 0.0 us)
Async XLA Ops:
  6.5 456.5 %copy-start = (f32[4]{0:T(128)S(1)}, f32[4]{0:T(128)}, u32[]{:S(2)}) copy-start(f32[4]{0:T(128)} %param.5) | copy-start | bytes 52
  6.5 701.9 %all-gather.2.cloned.1.call-start = ((), (), s32[]{:S(2)}) async-start(), calls=%async_computation.2 | async-start | bytes 51609600 | tf_op jit(solution)/shard_map/all_gather | solution.py:18
  442.0 21.3 %copy-start.2 = (f32[2000]{0:T(1024)S(1)}, f32[2000]{0:T(1024)}, u32[]{:S(2)}) copy-start(f32[2000]{0:T(1024)} %param.6) | copy-start | bytes 24004
  462.3 396.6 %reduce-scatter.2.cloned.1.call-start = ((), (), s32[]{:S(2)}) async-start(), calls=%async_computation.3 | async-start | bytes 8192000 | tf_op jit(solution)/shard_map/reduce_scatter | solution.py:22
  708.5 150.5 %copy-start.1 = (f32[4]{0:T(128)S(1)}, f32[4]{0:T(128)}, u32[]{:S(2)}) copy-start(f32[4]{0:T(128)} %param.5) | copy-start | bytes 52
Sparse Core Ops, SparseCore 0:
  462.5 245.9 all-gather.1
  744.0 115.0 reduce-scatter.1
where the time goes:
time: 869 us; the launch traced here: 866 us
  blocking collectives  367 us (42%)
  waiting for transfers between devices  360 us (41%)
  local copies, waits for them, and re-layouts  89.1 us (10%)
  matrix products  35.3 us (4%)
  between operations  14.1 us (2%)
    all_to_all x1, blocking collectives, local(): lax.all_to_all(three_center, 'pair', split_axis=2, concat_axis=0, tiled=T...  367 us
    all_gather x1, waiting for transfers between devices, local(): lax.all_gather(plain_rows, ('aux', 'rep'), axis=0, tiled=True)  245 us
    reduce_scatter x1, waiting for transfers between devices, local(): lax.psum_scatter(partial_sums, 'pair', scatter_dimension=1, tiled=True)  115 us
    all_to_all x2, local copies, waits for them, and re-layouts, local(): lax.all_to_all(three_center, 'pair', split_axis=2, concat_axis=0, tiled=T...  56 us
    dot_general x1, matrix products, local(): lax.dot_general(scaled, lax.all_gather(plain_rows, ('aux', 'rep'), axis=0...  35.3 us
    unnamed x7, local copies, waits for them, and re-layouts  32.8 us
  transfers between devices with their start and end apart: 2, of which 2 were waited for; matrix products, arithmetic and copies ran while one was open for 0% of the time, Pallas kernels for 0%

commit v1 on v0

--- a/solution.py
+++ b/solution.py
@@ -4,8 +4,30 @@
 from jax.sharding import PartitionSpec as P
 
 
+def split_up(x, dim, peers):
+    before, after = (x.shape[:dim], x.shape[dim + 1 :])
+    return jnp.moveaxis(x.reshape(*before, peers, -1, *after), dim, 0)
+
+
+def joined_along(blocks, dim):
+    blocks = jnp.moveaxis(blocks, 0, dim)
+    shape = blocks.shape
+    return blocks.reshape(*shape[:dim], shape[dim] * shape[dim + 1], *shape[dim + 2 :])
+
+
+def swapped_with_each(value, axis, split_dim, concat_dim):
+    length, index = (lax.axis_size(axis), lax.axis_index(axis))
+    parts = split_up(value, split_dim, length)
+    outs = [parts[index]]
+    for step in range(1, length):
+        sent = parts[index ^ step]
+        outs.append(lax.ppermute(sent, axis, [(i, i ^ step) for i in range(length)]))
+    parts = jnp.stack(outs)[index ^ jnp.arange(length)]
+    return joined_along(parts, concat_dim)
+
+
 def local(three_center, eps_occ, eps_virt, freq):
-    arrived = lax.all_to_all(three_center, "pair", split_axis=2, concat_axis=0, tiled=True)
+    arrived = swapped_with_each(three_center, "pair", 2, 0)
     excite = eps_virt[None, :] - eps_occ[:, None]
     weight = 2.0 * excite / (excite * excite + freq[0] * freq[0])
     height = arrived.shape[0]

time: 869 us -> 772 us (0.89)
  blocking collectives: 367 us -> 0 us
  waiting for transfers between devices: 360 us -> 576 us
  local copies, waits for them, and re-layouts: 89.1 us -> 131 us
    all_to_all x1 -> x0, blocking collectives: 367 us -> none  [local(): lax.all_to_all(three_center, 'pair', split_axis=2, concat_axis=0, tiled=T...]
    ppermute x0 -> x3, waiting for transfers between devices: none -> 215 us  [swapped_with_each(): lax.ppermute(sent, axis, [(i, i ^ step) for i in range(length)])]
    all_to_all x2 -> x0, local copies, waits for them, and re-layouts: 56 us -> none  [local(): lax.all_to_all(three_center, 'pair', split_axis=2, concat_axis=0, tiled=T...]
    reshape x0 -> x2, local copies, waits for them, and re-layouts: none -> 44.6 us  [the longest x1 24.2 us: split_up(): return jnp.moveaxis(x.reshape(*before, peers, -1, *after), dim, 0)]
    another operation x0 -> x1, local copies, waits for them, and re-layouts: none -> 33.1 us
    gather x0 -> x4, local copies, waits for them, and re-layouts: none -> 17.8 us  [swapped_with_each(): parts = jnp.stack(outs)[index ^ jnp.arange(length)]]
    unnamed x7 -> x11, local copies, waits for them, and re-layouts: 32.8 us -> 35.4 us
  transfers between devices with their start and end apart: 2 -> 5, of which waited for: 2 -> 5; matrix products, arithmetic and copies ran while one was open for 0% -> 1% of each run, Pallas kernels for 0% -> 0%
where the time goes in v1:
time: 772 us; the launch traced here: 771 us
  waiting for transfers between devices  576 us (75%)
  local copies, waits for them, and re-layouts  131 us (17%)
  matrix products  35.5 us (5%)
  between operations  14.2 us (2%)
    all_gather x1, waiting for transfers between devices, local(): lax.all_gather(plain_rows, ('aux', 'rep'), axis=0, tiled=True)  246 us
    ppermute x3, waiting for transfers between devices, swapped_with_each(): lax.ppermute(sent, axis, [(i, i ^ step) for i in range(length)])  215 us
    reduce_scatter x1, waiting for transfers between devices, local(): lax.psum_scatter(partial_sums, 'pair', scatter_dimension=1, tiled=True)  115 us
    dot_general x1, matrix products, local(): lax.dot_general(scaled, lax.all_gather(plain_rows, ('aux', 'rep'), axis=0...  35.5 us
    unnamed x11, local copies, waits for them, and re-layouts  35.4 us
    another operation x1, local copies, waits for them, and re-layouts  33.1 us
    reshape x1, local copies, waits for them, and re-layouts, split_up(): return jnp.moveaxis(x.reshape(*before, peers, -1, *after), dim, 0)  24.2 us
    reshape x1, local copies, waits for them, and re-layouts, joined_along(): blocks.reshape(*shape[:dim], shape[dim] * shape[dim + 1], *shape[dim + 2:])  20.3 us
  transfers between devices with their start and end apart: 5, of which 5 were waited for; matrix products, arithmetic and copies ran while one was open for 1% of the time, Pallas kernels for 0%

profile of v1, /device:TPU:0, one launch (start us, length us, event | category | flops | bytes accessed | tf_op | source)
XLA Modules:
  0.0 770.5 jit_solution(17815522248175711828)
XLA Ops:
  6.5 24.2 %reshape.79 = bf16[160,4,4,2000]{3,2,1,0:T(4,128)(2,1)} reshape(bf16[160,4,8000]{2,1,0:T(4,128)(2,1)} %param.4) | data formatting | bytes 20480000 | tf_op jit(solution)/shard_map/reshape | solution.py:9
  30.8 33.1 %constant_dynamic-slice_fusion.3 = (bf16[160,4,1,2000]{3,2,1,0:T(2,128)(2,1)S(1)}, bf16[160,4,1,2000]{3,2,1,0:T(2,128)(2,1)S(1)}, bf16[160,4,1,2000]{3,2,1,0:T(2,128)(2,1)S(1)}, bf16[160,4,1,2000]{3,2,1,0:T(2,128)(2,1)S(1)}) fusion(bf16[160,4,4,2000]{3,2,1,0:T(4,128)(2,1)} %reshape.79, s32[]{:T(128)S(6)} %select_n.22, s32[]{:T(128)S(6)} %select_n.24, ...), kind=kLoop, calls=%fused_computation.18 | loop fusion | bytes 20480016 | tf_op jit(solution)/shard_map/dynamic-slice
  63.9 2.8 copy.33
  66.7 5.1 collective-permute-start.2
  71.8 2.8 copy.35
  74.7 2.8 copy.34
  77.5 0.6 collective-permute-start.1
  78.1 2.8 copy.36
  80.9 0.2 pad_clamp_fusion
  81.2 48.4 %collective-permute-done.2 = bf16[160,4,2000]{2,0,1:T(8,128)(2,1)S(1)} collective-permute-done((bf16[160,4,2000]{2,0,1:T(8,128)(2,1)S(1)}, bf16[160,4,2000]{2,0,1:T(8,128)(2,1)S(1)}, u32[]{:S(2)}, u32[]{:S(2)}) %collective-permute-start.2) | collective-permute-done | bytes 2560032 | tf_op jit(solution)/shard_map/ppermute | solution.py:24
  129.6 56.4 %collective-permute-done = bf16[160,4,2000]{2,0,1:T(8,128)(2,1)S(1)} collective-permute-done((bf16[160,4,2000]{2,0,1:T(8,128)(2,1)S(1)}, bf16[160,4,2000]{2,0,1:T(8,128)(2,1)S(1)}, u32[]{:S(2)}, u32[]{:S(2)}) %collective-permute-start) | collective-permute-done | bytes 2560032 | tf_op jit(solution)/shard_map/ppermute | solution.py:24
  186.0 110.4 %collective-permute-done.1 = bf16[160,4,2000]{2,0,1:T(8,128)(2,1)S(1)} collective-permute-done((bf16[160,4,2000]{2,0,1:T(8,128)(2,1)S(1)}, bf16[160,4,2000]{2,0,1:T(8,128)(2,1)S(1)}, u32[]{:S(2)}, u32[]{:S(2)}) %collective-permute-start.1) | collective-permute-done | bytes 2560032 | tf_op jit(solution)/shard_map/ppermute | solution.py:24
  296.4 1.4 pad_maximum_fusion
  297.8 3.2 mini-gather-slice.2
  301.0 3.2 mini-gather-slice.3
  304.2 5.7 gather_fusion.1
  309.9 5.7 gather_fusion
  315.6 5.7 pad_maximum_fusion.1
  321.3 24.2 %copy.7 = bf16[4,160,4,2000]{3,2,1,0:T(4,128)(2,1)} copy(bf16[4,160,4,2000]{3,1,2,0:T(8,128)(2,1)S(1)} %pad_maximum_fusion.1) | data formatting | bytes 20480000
  345.5 20.3 %reshape.62 = bf16[640,8000]{1,0:T(8,128)(2,1)} reshape(bf16[4,160,4,2000]{3,2,1,0:T(4,128)(2,1)} %copy.7) | data formatting | bytes 20480000 | tf_op jit(solution)/shard_map/reshape | solution.py:15
  366.6 0.1 broadcast_reduce_fusion
  366.9 246.1 %all-gather.2.cloned.1.call-done = bf16[2560,8000]{1,0:T(8,128)(2,1)} async-done(((bf16[640,8000]{1,0:T(8,128)(2,1)}), bf16[2560,8000]{1,0:T(8,128)(2,1)}) %all-gather.2.cloned.1.call-update) | async-done | bytes 40960016 | tf_op jit(solution)/shard_map/all_gather | solution.py:40
  613.0 35.5 %fusion = f32[640,2560]{1,0:T(8,128)} fusion(bf16[2560,8000]{1,0:T(8,128)(2,1)} %all-gather.2.cloned.1.call-done, bf16[640,8000]{1,0:T(8,128)(2,1)} %reshape.62, f32[8000]{0:T(1024)S(1)} %add_divide_fusion), kind=kOutput, calls=%fused_computation.5 | convolution fusion | flops 26229760000 | bytes 57785600 | tf_op jit(solution)/shard_map/dot_general | solution.py:38
  648.5 115.2 %reduce-scatter.2.cloned.1.call-done = f32[640,640]{1,0:T(8,128)} async-done(((f32[640,2560]{1,0:T(8,128)}), f32[640,640]{1,0:T(8,128)}) %reduce-scatter.2.cloned.1.call-update) | async-done | bytes 1638416 | tf_op jit(solution)/shard_map/reduce_scatter | solution.py:44
  (16 shorter events, 0.4 us)
Async XLA Ops:
  6.5 360.1 %copy-start = (f32[4]{0:T(128)S(1)}, f32[4]{0:T(128)}, u32[]{:S(2)}) copy-start(f32[4]{0:T(128)} %param.5) | copy-start | bytes 52
  6.5 606.5 %all-gather.2.cloned.1.call-start = ((), (), s32[]{:S(2)}) async-start(), calls=%async_computation.1 | async-start | bytes 51609600 | tf_op jit(solution)/shard_map/all_gather | solution.py:40
  66.7 62.9 %collective-permute-start.2 = (bf16[160,4,2000]{2,0,1:T(8,128)(2,1)S(1)}, bf16[160,4,2000]{2,0,1:T(8,128)(2,1)S(1)}, u32[]{:S(2)}, u32[]{:S(2)}) collective-permute-start(bf16[160,4,2000]{2,0,1:T(8,128)(2,1)S(1)} %bitcast.27), channel_id=1, source_target_pairs={{0,12},{4,8},{8,4},{12,0},{1,13},{5,9},{9,5},{13,1},{2,14},{6,10},... | collective-permute-start | bytes 7680008 | tf_op jit(solution)/shard_map/ppermute | solution.py:24
  74.6 111.4 %collective-permute-start = (bf16[160,4,2000]{2,0,1:T(8,128)(2,1)S(1)}, bf16[160,4,2000]{2,0,1:T(8,128)(2,1)S(1)}, u32[]{:S(2)}, u32[]{:S(2)}) collective-permute-start(bf16[160,4,2000]{2,0,1:T(8,128)(2,1)S(1)} %bitcast.28), channel_id=1, source_target_pairs={{0,4},{4,0},{8,12},{12,8},{1,5},{5,1},{9,13},{13,9},{2,6},{6,2},{1... | collective-permute-start | bytes 7680008 | tf_op jit(solution)/shard_map/ppermute | solution.py:24
  77.5 218.9 %collective-permute-start.1 = (bf16[160,4,2000]{2,0,1:T(8,128)(2,1)S(1)}, bf16[160,4,2000]{2,0,1:T(8,128)(2,1)S(1)}, u32[]{:S(2)}, u32[]{:S(2)}) collective-permute-start(bf16[160,4,2000]{2,0,1:T(8,128)(2,1)S(1)} %bitcast.29), channel_id=1, source_target_pairs={{0,8},{4,12},{8,0},{12,4},{1,9},{5,13},{9,1},{13,5},{2,10},{6,14},... | collective-permute-start | bytes 7680008 | tf_op jit(solution)/shard_map/ppermute | solution.py:24
  365.9 0.9 copy-start.2
  365.9 397.8 %reduce-scatter.2.cloned.1.call-start = ((), (), s32[]{:S(2)}) async-start(), calls=%async_computation.2 | async-start | bytes 8192000 | tf_op jit(solution)/shard_map/reduce_scatter | solution.py:44
  613.0 150.7 %copy-start.1 = (f32[4]{0:T(128)S(1)}, f32[4]{0:T(128)}, u32[]{:S(2)}) copy-start(f32[4]{0:T(128)} %param.5) | copy-start | bytes 52
Sparse Core Ops, SparseCore 0:
  366.0 246.9 all-gather.1
  648.6 115.0 reduce-scatter.1
